TPU v7x, 32 devices: a whole 2x2x4 slice. The times are simulated.
32 devices in a mesh: group: 4 (over y, x), seq: 4 (over z), hid: 2 (over core).
Axes of the slice: x: 2, y: 2, z: 4, core: 2. Of those that a mesh axis runs over, the one named last changes fastest.
Arguments:
- tokens: bfloat16 [4, 8192, 1280], P('group', ('seq', 'hid')), may hold values from -6 to 6
- slot_embed: bfloat16 [1280, 16], replicated, may hold values from -6 to 6
- seq_lengths: int32 [4, 8], P('group'), may hold values from 1 to 2048, 8192 in all within a row
- w_in: bfloat16 [8, 1280, 2560], P(('seq', 'hid'), None, 'group'), may hold values from -0.3125 to 0.3125
- w_out: bfloat16 [8, 2560, 1280], P(('seq', 'hid'), 'group'), may hold values from -0.25 to 0.25
Outputs:
- mixed: bfloat16 [4, 8192, 1280], P('group', ('seq', 'hid'))
Inputs may be any that keep to these rules, and one draw needn't show every extreme that they name: `seq_lengths`: each row sums to 8192; its largest entry is 2048.
All inputs are finite; a program needn't handle non-finite values.
Results may differ from a plain program's by a relative error of at most 0.013.
Values may be sent and summed in bfloat16 or wider, within the bound.
No kernel may reach another device: no remote copies, remote signals or barrier semaphores. Data moves between devices by JAX's collectives and lax.ppermute only.
A program may use at most 64 MiB of HBM per device.

v0:
```python
import jax
import jax.numpy as jnp
from jax import lax
from jax.sharding import PartitionSpec as P


def body(tokens, slot_embed, seq_lengths, w_in, w_out):
    local_tokens = tokens[0]
    tok_count = local_tokens.shape[0]
    shard_index = lax.axis_index("seq") * lax.axis_size("hid") + lax.axis_index("hid")
    position = shard_index * tok_count + jnp.arange(tok_count, dtype=jnp.int32)
    seq_end = jnp.cumsum(seq_lengths[0])
    seq_start = seq_end - seq_lengths[0]
    member = (position[:, None] >= seq_start[None, :]) & (position[:, None] < seq_end[None, :])
    member_f = member.astype(jnp.float32)
    seq_count = member.shape[1]
    highest = lax.Precision.HIGHEST
    logits = jnp.dot(local_tokens, slot_embed, preferred_element_type=jnp.float32)
    slot_count = logits.shape[1]
    masked = jnp.where(member[:, :, None], logits[:, None, :], -1e30)
    local_peak = jnp.max(masked, axis=0)
    seq_peak = lax.pmax(local_peak, ("seq", "hid"))
    token_peak = jnp.dot(member_f, seq_peak, precision=highest)
    exponent = jnp.exp(logits - token_peak)
    seq_total = lax.psum(jnp.dot(member_f.T, exponent, precision=highest), ("seq", "hid"))
    token_total = jnp.dot(member_f, seq_total, precision=highest)
    weights = exponent / token_total
    dispatch = (
        (weights[:, :, None] * member_f[:, None, :])
        .astype(jnp.bfloat16)
        .reshape(tok_count, slot_count * seq_count)
    )
    columns = dispatch
    own_rows = lax.psum_scatter(
        lax.dot_general(
            columns, local_tokens, (((0,), (0,)), ((), ())), preferred_element_type=jnp.float32
        ),
        ("seq", "hid"),
        scatter_dimension=0,
        tiled=True,
    )
    slot_inputs = own_rows.astype(jnp.bfloat16)
    hidden = jax.nn.gelu(
        jnp.dot(
            lax.all_gather(slot_inputs, "group", axis=0, tiled=True),
            w_in[0],
            preferred_element_type=jnp.float32,
        ),
        approximate=True,
    ).astype(jnp.bfloat16)
    partial_out = jnp.dot(hidden, w_out[0], preferred_element_type=jnp.float32)
    slot_outputs = lax.psum_scatter(
        partial_out.astype(jnp.bfloat16), "group", scatter_dimension=0, tiled=True
    )
    mix_weights = jax.nn.softmax(logits, axis=1)
    slot_table = (
        (mix_weights[:, :, None] * member_f[:, None, :])
        .astype(jnp.bfloat16)
        .reshape(tok_count, slot_count * seq_count)
    )
    block_rows = lax.all_gather(slot_outputs[None], ("seq", "hid"), axis=0, tiled=True)
    col_width = block_rows.shape[0] * block_rows.shape[1]
    columns = slot_table
    mixed = jnp.dot(
        columns,
        block_rows.reshape(col_width, block_rows.shape[2]),
        preferred_element_type=jnp.float32,
    )
    return mixed.astype(jnp.bfloat16)[None]


def solution(mesh):
    placed = (
        P("group", ("seq", "hid"), None),
        P(),
        P("group", None),
        P(("seq", "hid"), None, "group"),
        P(("seq", "hid"), "group", None),
    )
    return jax.shard_map(
        body,
        mesh=mesh,
        in_specs=placed,
        out_specs=P("group", ("seq", "hid"), None),
        check_vma=False,
    )
```

profile of v0, /device:TPU:0, one launch (start us, length us, event | category | flops | bytes accessed | tf_op | source)
XLA Modules:
  0.0 132.2 jit_solution(14160902849086294041)
XLA Ops:
  6.5 0.0 copy-start
  6.5 0.0 reduce-scatter.3.cloned.1.call-start
  6.5 1.0 reduce-window.4
  7.5 0.7 fusion.37
  8.2 0.1 copy-done
  8.3 1.6 %fusion.44 = (f32[1024]{0:T(1024)S(1)}, f32[1024,16]{0,1:T(8,128)S(1)}) fusion(bf16[1280,16]{0,1:T(8,128)(2,1)} %param.6, bf16[1,1024,1280]{2,1,0:T(8,128)(2,1)S(1)} %copy-done), kind=kOutput, calls=%fused_computation.48 | convolution fusion | flops 41958400 | bytes 2732032 | tf_op jit(solution)/shard_map/dot_general | solution.py:18
  9.9 0.1 fusion.43
  10.0 0.1 select_reduce_fusion
  10.1 18.1 %pmax.7 = f32[8,16]{1,0:T(8,128)S(1)} all-reduce(f32[8,16]{1,0:T(8,128)S(1)} %select_reduce_fusion), channel_id=1, replica_groups=mesh['group'=4,'seq'=4,'hid'=2] {'seq','hid'}, use_global_device_ids=true, to_apply=%region_4.5 | all-reduce | flops 128 | bytes 1024 | tf_op jit(solution)/shard_map/pmax | solution.py:22
  28.2 0.3 fusion.8
  28.5 0.2 fusion.42
  28.6 13.6 %psum.7 = f32[8,16]{1,0:T(8,128)S(1)} all-reduce(f32[8,16]{1,0:T(8,128)S(1)} %fusion.42), channel_id=1, replica_groups=mesh['group'=4,'seq'=4,'hid'=2] {'seq','hid'}, use_global_device_ids=true, to_apply=%region_5.6 | all-reduce | flops 128 | bytes 1024 | tf_op jit(solution)/shard_map/psum | solution.py:25
  42.3 0.3 convolution_divide_fusion
  42.5 1.4 %fusion.1 = f32[128,1280]{1,0:T(8,128)} fusion(bf16[1,1024,1280]{2,1,0:T(8,128)(2,1)S(1)} %copy-done, f32[1024,16]{0,1:T(8,128)S(1)} %convolution_divide_fusion, f32[1024,8]{0,1:T(8,128)S(1)} %get-tuple-element.5), kind=kOutput, calls=%fused_computation.2 | convolution fusion | flops 335806464 | bytes 3375104 | tf_op jit(solution)/shard_map/dot_general | solution.py:35
  43.9 0.0 reduce-scatter.3.cloned.1.call-update
  43.9 0.0 reduce-scatter.5.cloned.1.call-start
  43.9 29.9 %reduce-scatter.3.cloned.1.call-done = f32[16,1280]{1,0:T(8,128)} async-done(((f32[128,1280]{1,0:T(8,128)}), f32[16,1280]{1,0:T(8,128)}) %reduce-scatter.3.cloned.1.call-update) | async-done | bytes 81936 | tf_op jit(solution)/shard_map/reduce_scatter | solution.py:34
  73.9 0.9 convert_element_type.50
  74.8 8.7 %all_gather.6 = bf16[64,1280]{1,0:T(8,128)(2,1)S(1)} all-gather(bf16[16,1280]{1,0:T(8,128)(2,1)S(1)} %convert_element_type.50), channel_id=1, replica_groups=mesh['group'=4,'seq'=4,'hid'=2] {'group'}, dimensions={0}, use_global_device_ids=true | all-gather | bytes 204800 | tf_op jit(solution)/shard_map/all_gather | solution.py:45
  83.4 3.4 %convolution_convert_fusion.1 = bf16[64,1280]{1,0:T(8,128)(2,1)} fusion(bf16[1,640,1280]{2,1,0:T(8,128)(2,1)} %param.9, bf16[64,1280]{1,0:T(8,128)(2,1)S(1)} %all_gather.6, bf16[1,1280,640]{2,1,0:T(8,128)(2,1)} %param.8), kind=kOutput, calls=%fused_computation.6 | convolution fusion | flops 210165760 | bytes 3604480 | tf_op jit(solution)/shard_map/dot_general | solution.py:51
  86.8 0.0 reduce-scatter.5.cloned.1.call-update
  86.9 21.5 %reduce-scatter.5.cloned.1.call-done = bf16[16,1280]{1,0:T(8,128)(2,1)} async-done(((bf16[64,1280]{1,0:T(8,128)(2,1)}), bf16[16,1280]{1,0:T(8,128)(2,1)}) %reduce-scatter.5.cloned.1.call-update) | async-done | bytes 40976 | tf_op jit(solution)/shard_map/reduce_scatter | solution.py:52
  108.5 14.6 %all-gather = bf16[128,1280]{1,0:T(8,128)(2,1)S(1)} all-gather(bf16[16,1280]{1,0:T(8,128)(2,1)} %reduce-scatter.5.cloned.1.call-done), channel_id=2, replica_groups=mesh['group'=4,'seq'=4,'hid'=2] {'seq','hid'}, dimensions={0}, use_global_device_ids=true | all-gather | bytes 368640 | tf_op jit(solution)/shard_map/all_gather | solution.py:61
  123.0 2.4 %fusion = bf16[1,1024,1280]{2,1,0:T(8,128)(2,1)} fusion(bf16[128,1280]{1,0:T(8,128)(2,1)S(1)} %all-gather, f32[1024,8]{0,1:T(8,128)S(1)} %get-tuple-element.5, f32[1024,16]{0,1:T(8,128)S(1)} %fusion.35), kind=kOutput, calls=%fused_computation.1 | convolution fusion | flops 337117184 | bytes 3047424 | tf_op jit(solution)/shard_map/dot_general | solution.py:64
  (3 shorter events, 0.1 us)
Async XLA Ops:
  6.5 1.8 %copy-start = (bf16[1,1024,1280]{2,1,0:T(8,128)(2,1)S(1)}, bf16[1,1024,1280]{2,1,0:T(8,128)(2,1)}, u32[]{:S(2)}) copy-start(bf16[1,1024,1280]{2,1,0:T(8,128)(2,1)} %param.5) | copy-start | bytes 7864324
  6.5 67.3 %reduce-scatter.3.cloned.1.call-start = ((), (), s32[]{:S(2)}) async-start(), calls=%async_computation.2 | async-start | bytes 737280 | tf_op jit(solution)/shard_map/reduce_scatter | solution.py:34
  43.9 64.6 %reduce-scatter.5.cloned.1.call-start = ((), (), s32[]{:S(2)}) async-start(), calls=%async_computation.3 | async-start | bytes 204800 | tf_op jit(solution)/shard_map/reduce_scatter | solution.py:52
Sparse Core Ops, SparseCore 0:
  44.0 29.8 reduce-scatter.2
  87.0 21.4 reduce-scatter.4
where the time goes:
time: 133 us; the launch traced here: 132 us
  blocking collectives  55 us (41%)
  waiting for transfers between devices  51.5 us (39%)
  between operations  13.5 us (10%)
  matrix products  9.39 us (7%)
  other arithmetic  2.79 us (2%)
    reduce_scatter x1, waiting for transfers between devices, body(): lax.psum_scatter(lax.dot_general(columns, local_tokens, (((0,), (0,)), ((...  29.9 us
    reduce_scatter x1, waiting for transfers between devices, body(): lax.psum_scatter(partial_out.astype(jnp.bfloat16), 'group', scatter_dimen...  21.5 us
    pmax x1, blocking collectives, body(): seq_peak = lax.pmax(local_peak, ('seq', 'hid'))  18.1 us
    all_gather x1, blocking collectives, body(): lax.all_gather(slot_outputs[None], ('seq', 'hid'), axis=0, tiled=True)  14.6 us
    psum x1, blocking collectives, body(): lax.psum(jnp.dot(member_f.T, exponent, precision=highest), ('seq', 'hid'))  13.6 us
    all_gather x1, blocking collectives, body(): lax.all_gather(slot_inputs, 'group', axis=0, tiled=True)  8.66 us
    dot_general x1, matrix products, body(): partial_out = jnp.dot(hidden, w_out[0], preferred_element_type=jnp.float32)  3.4 us
  transfers between devices with their start and end apart: 2, of which 2 were waited for; matrix products, arithmetic and copies ran while one was open for 0% of the time, Pallas kernels for 0%

commit v1 on v0

--- a/solution.py
+++ b/solution.py
@@ -22,7 +22,9 @@
     seq_peak = lax.pmax(local_peak, ("seq", "hid"))
     token_peak = jnp.dot(member_f, seq_peak, precision=highest)
     exponent = jnp.exp(logits - token_peak)
-    seq_total = lax.psum(jnp.dot(member_f.T, exponent, precision=highest), ("seq", "hid"))
+    own = jnp.dot(member_f.T, exponent, precision=highest)
+    parts = lax.all_gather(own, ("seq", "hid"), axis=0, tiled=False)
+    seq_total = parts.sum(axis=0)
     token_total = jnp.dot(member_f, seq_total, precision=highest)
     weights = exponent / token_total
     dispatch = (

time: 133 us -> 133 us (level)
    all_gather x0 -> x1, blocking collectives: none -> 14.1 us  [body(): parts = lax.all_gather(own, ('seq', 'hid'), axis=0, tiled=False)]
    psum x1 -> x0, blocking collectives: 13.6 us -> none  [body(): lax.psum(jnp.dot(member_f.T, exponent, precision=highest), ('seq', 'hid'))]
where the time goes in v1:
time: 133 us
  blocking collectives  55.5 us (42%)
  waiting for transfers between devices  51.4 us (39%)
  between operations  13.5 us (10%)
  matrix products  9.38 us (7%)
  other arithmetic  2.8 us (2%)
    reduce_scatter x1, waiting for transfers between devices, body(): lax.psum_scatter(lax.dot_general(columns, local_tokens, (((0,), (0,)), ((...  29.9 us
    reduce_scatter x1, waiting for transfers between devices, body(): lax.psum_scatter(partial_out.astype(jnp.bfloat16), 'group', scatter_dimen...  21.5 us
    pmax x1, blocking collectives, body(): seq_peak = lax.pmax(local_peak, ('seq', 'hid'))  18.1 us
    all_gather x1, blocking collectives, body(): lax.all_gather(slot_outputs[None], ('seq', 'hid'), axis=0, tiled=True)  14.6 us
    all_gather x1, blocking collectives, body(): parts = lax.all_gather(own, ('seq', 'hid'), axis=0, tiled=False)  14.1 us
    all_gather x1, blocking collectives, body(): lax.all_gather(slot_inputs, 'group', axis=0, tiled=True)  8.67 us
    dot_general x1, matrix products, body(): partial_out = jnp.dot(hidden, w_out[0], preferred_element_type=jnp.float32)  3.39 us
  transfers between devices with their start and end apart: 2, of which 2 were waited for; matrix products, arithmetic and copies ran while one was open for 0% of the time, Pallas kernels for 0%

profile of v1, /device:TPU:0, one launch (start us, length us, event | category | flops | bytes accessed | tf_op | source)
XLA Modules:
  0.0 132.7 jit_solution(4319129441120626156)
XLA Ops:
  6.5 0.0 copy-start
  6.5 0.0 reduce-scatter.3.cloned.1.call-start
  6.5 1.0 reduce-window.4
  7.5 0.7 fusion.37
  8.2 0.1 copy-done
  8.3 1.6 %fusion.44 = (f32[1024]{0:T(1024)S(1)}, f32[1024,16]{0,1:T(8,128)S(1)}) fusion(bf16[1280,16]{0,1:T(8,128)(2,1)} %param.6, bf16[1,1024,1280]{2,1,0:T(8,128)(2,1)S(1)} %copy-done), kind=kOutput, calls=%fused_computation.49 | convolution fusion | flops 41958400 | bytes 2732032 | tf_op jit(solution)/shard_map/dot_general | solution.py:18
  9.9 0.1 fusion.43
  10.0 0.1 select_reduce_fusion
  10.1 18.1 %pmax.7 = f32[8,16]{1,0:T(8,128)S(1)} all-reduce(f32[8,16]{1,0:T(8,128)S(1)} %select_reduce_fusion), channel_id=1, replica_groups=mesh['group'=4,'seq'=4,'hid'=2] {'seq','hid'}, use_global_device_ids=true, to_apply=%region_4.5 | all-reduce | flops 128 | bytes 1024 | tf_op jit(solution)/shard_map/pmax | solution.py:22
  28.2 0.3 fusion.8
  28.5 0.2 fusion.42
  28.6 14.1 %all-gather = f32[64,16]{1,0:T(8,128)S(1)} all-gather(f32[8,16]{1,0:T(8,128)S(1)} %fusion.42), channel_id=2, replica_groups=mesh['group'=4,'seq'=4,'hid'=2] {'seq','hid'}, dimensions={0}, use_global_device_ids=true | all-gather | bytes 4608 | tf_op jit(solution)/shard_map/all_gather | solution.py:26
  42.8 0.3 convolution_divide_fusion
  43.0 1.4 %fusion.1 = f32[128,1280]{1,0:T(8,128)} fusion(bf16[1,1024,1280]{2,1,0:T(8,128)(2,1)S(1)} %copy-done, f32[1024,16]{0,1:T(8,128)S(1)} %convolution_divide_fusion, f32[1024,8]{0,1:T(8,128)S(1)} %get-tuple-element.5), kind=kOutput, calls=%fused_computation.2 | convolution fusion | flops 335806464 | bytes 3375104 | tf_op jit(solution)/shard_map/dot_general | solution.py:37
  44.4 0.0 reduce-scatter.3.cloned.1.call-update
  44.4 0.0 reduce-scatter.5.cloned.1.call-start
  44.5 29.9 %reduce-scatter.3.cloned.1.call-done = f32[16,1280]{1,0:T(8,128)} async-done(((f32[128,1280]{1,0:T(8,128)}), f32[16,1280]{1,0:T(8,128)}) %reduce-scatter.3.cloned.1.call-update) | async-done | bytes 81936 | tf_op jit(solution)/shard_map/reduce_scatter | solution.py:36
  74.3 0.9 convert_element_type.50
  75.2 8.7 %all_gather.14 = bf16[64,1280]{1,0:T(8,128)(2,1)S(1)} all-gather(bf16[16,1280]{1,0:T(8,128)(2,1)S(1)} %convert_element_type.50), channel_id=1, replica_groups=mesh['group'=4,'seq'=4,'hid'=2] {'group'}, dimensions={0}, use_global_device_ids=true | all-gather | bytes 204800 | tf_op jit(solution)/shard_map/all_gather | solution.py:47
  83.9 3.4 %convolution_convert_fusion.1 = bf16[64,1280]{1,0:T(8,128)(2,1)} fusion(bf16[1,640,1280]{2,1,0:T(8,128)(2,1)} %param.9, bf16[64,1280]{1,0:T(8,128)(2,1)S(1)} %all_gather.14, bf16[1,1280,640]{2,1,0:T(8,128)(2,1)} %param.8), kind=kOutput, calls=%fused_computation.6 | convolution fusion | flops 210165760 | bytes 3604480 | tf_op jit(solution)/shard_map/dot_general | solution.py:53
  87.3 0.0 reduce-scatter.5.cloned.1.call-update
  87.4 21.5 %reduce-scatter.5.cloned.1.call-done = bf16[16,1280]{1,0:T(8,128)(2,1)} async-done(((bf16[64,1280]{1,0:T(8,128)(2,1)}), bf16[16,1280]{1,0:T(8,128)(2,1)}) %reduce-scatter.5.cloned.1.call-update) | async-done | bytes 40976 | tf_op jit(solution)/shard_map/reduce_scatter | solution.py:54
  108.9 14.6 %all-gather.1 = bf16[128,1280]{1,0:T(8,128)(2,1)S(1)} all-gather(bf16[16,1280]{1,0:T(8,128)(2,1)} %reduce-scatter.5.cloned.1.call-done), channel_id=3, replica_groups=mesh['group'=4,'seq'=4,'hid'=2] {'seq','hid'}, dimensions={0}, use_global_device_ids=true | all-gather | bytes 368640 | tf_op jit(solution)/shard_map/all_gather | solution.py:63
  123.5 2.4 %fusion = bf16[1,1024,1280]{2,1,0:T(8,128)(2,1)} fusion(bf16[128,1280]{1,0:T(8,128)(2,1)S(1)} %all-gather.1, f32[1024,8]{0,1:T(8,128)S(1)} %get-tuple-element.5, f32[1024,16]{0,1:T(8,128)S(1)} %fusion.35), kind=kOutput, calls=%fused_computation.1 | convolution fusion | flops 337117184 | bytes 3047424 | tf_op jit(solution)/shard_map/dot_general | solution.py:66
  (4 shorter events, 0.1 us)
Async XLA Ops:
  6.5 1.8 %copy-start = (bf16[1,1024,1280]{2,1,0:T(8,128)(2,1)S(1)}, bf16[1,1024,1280]{2,1,0:T(8,128)(2,1)}, u32[]{:S(2)}) copy-start(bf16[1,1024,1280]{2,1,0:T(8,128)(2,1)} %param.5) | copy-start | bytes 7864324
  6.5 67.8 %reduce-scatter.3.cloned.1.call-start = ((), (), s32[]{:S(2)}) async-start(), calls=%async_computation.2 | async-start | bytes 737280 | tf_op jit(solution)/shard_map/reduce_scatter | solution.py:36
  44.4 64.5 %reduce-scatter.5.cloned.1.call-start = ((), (), s32[]{:S(2)}) async-start(), calls=%async_computation.3 | async-start | bytes 204800 | tf_op jit(solution)/shard_map/reduce_scatter | solution.py:54
Sparse Core Ops, SparseCore 0:
  44.5 29.7 reduce-scatter.2
  87.4 21.4 reduce-scatter.4
